TPU v7x, 256 devices: a whole 4x4x8 slice. The times are simulated.
256 devices in a mesh: segment: 4 (over y_lo, core), dp: 64 (over z, x, y_hi).
Axes of the slice: x: 4, y: 4 (y_hi: 2, y_lo: 2; y = y_hi * 2 + y_lo), z: 8, core: 2. Of those that a mesh axis runs over, the one named last changes fastest.
Arguments:
- images: bfloat16 [512, 256, 1024], P('dp'), may hold values from -6 to 6
- texts: bfloat16 [512, 64, 1536], P('dp'), may hold values from -6 to 6
- section_weights: bfloat16 [4, 21504, 128], P('segment'), may hold values from -0.15625 to 0.15625
- uniting_weights: bfloat16 [3584, 1024], P('dp'), may hold values from -0.125 to 0.125
- codebooks: float32 [64, 2, 256, 1024], P('dp'), may hold values from -3 to 3
- neg_bank: bfloat16 [64, 256, 1024], P('dp'), may hold values from -6 to 6
- item_cats: int32 [4, 128, 1], replicated, may hold values from 0 to 63; in each aligned block of 128 rows (0 to 127, 128 to 255, ..., all dimensions but the last counted through in order) at most 2 rows name the same one
- cat_slot: int32 [64], replicated, may hold values from 0 to 63, each once
- neg_index: int32 [4, 128, 128], replicated, may hold values from 0 to 255
Outputs:
- uniting_grad: float32 [3584, 1024], P('dp')
- codebook_grad: float32 [64, 2, 256, 1024], P('dp')
- owner_loss: float32 [64], P('dp')
Inputs may be any that keep to these rules, and one draw needn't show every extreme that they name: `item_cats`: within one row of 128 no category appears more than 2 times, and in some row some category appears exactly 2 times. `cat_slot`: A permutation: every category has its own slot; slot t lies with owner t.
All inputs are finite; a program needn't handle non-finite values.
Results may differ from a plain program's by a relative error of at most 0.028.
Values may be sent and summed in bfloat16 or wider, within the bound.
A program may use at most 128 MiB of HBM per device.

v0:
```python
import math
import jax
import jax.numpy as jnp
from jax import lax
from jax.sharding import PartitionSpec as P

HEAD_IMG = 64
HEAD_TXT = 128
CAP = 2
norm_eps = 1e-06
rope_theta = 1000000.0
contrast_temp = 0.1
beta_weight = 1.0
highest = lax.Precision.HIGHEST


def gelu_value(inputs_f):
    return 0.5 * inputs_f * (1.0 + lax.erf(inputs_f / math.sqrt(2.0)))


def gelu_slope(inputs_f):
    return 0.5 * (1.0 + lax.erf(inputs_f / math.sqrt(2.0))) + inputs_f * jnp.exp(
        -0.5 * inputs_f * inputs_f
    ) / math.sqrt(2.0 * math.pi)


def rotate_pairs(tensor, positions):
    half_dim = tensor.shape[-1] // 2
    exponents = jnp.arange(half_dim).astype(jnp.float32) * (2.0 / tensor.shape[-1])
    inverse_freq = jnp.exp(-math.log(rope_theta) * exponents)
    angles = positions[:, None] * inverse_freq[None, :]
    cosine = jnp.concatenate([jnp.cos(angles), jnp.cos(angles)], axis=-1)[:, None, :]
    sine = jnp.concatenate([jnp.sin(angles), jnp.sin(angles)], axis=-1)[:, None, :]
    rotated = jnp.concatenate([-tensor[..., half_dim:], tensor[..., :half_dim]], axis=-1)
    return tensor * cosine + rotated * sine


def softmax_rows(scores):
    scores = scores - jnp.max(scores, axis=-1, keepdims=True)
    exp_scores = jnp.exp(scores)
    return (exp_scores / jnp.sum(exp_scores, axis=-1, keepdims=True)).astype(jnp.bfloat16)


def image_attention(images, flat_slot):
    item_count, patch_count, model_width = images.shape
    half_width = model_width // 2
    head_count = half_width // HEAD_IMG
    qkv_size = model_width * 3 * half_width
    w_qkv = flat_slot[:qkv_size].reshape(model_width, 3 * half_width)
    w_out = flat_slot[qkv_size : qkv_size + half_width * model_width].reshape(
        half_width, model_width
    )
    float_tokens = images.astype(jnp.float32)
    centred = float_tokens - jnp.mean(float_tokens, axis=-1, keepdims=True)
    variance = jnp.mean(centred * centred, axis=-1, keepdims=True)
    normed = (centred * lax.rsqrt(variance + norm_eps)).astype(jnp.bfloat16)
    projections = jnp.einsum(
        "bpd,de->bpe", normed, w_qkv, preferred_element_type=jnp.float32
    ).astype(jnp.bfloat16)
    queries = projections[..., :half_width].reshape(item_count, patch_count, head_count, HEAD_IMG)
    key_rows = projections[..., half_width : 2 * half_width].reshape(
        item_count, patch_count, head_count, HEAD_IMG
    )
    value_rows = projections[..., 2 * half_width :].reshape(
        item_count, patch_count, head_count, HEAD_IMG
    )
    scores = jnp.einsum(
        "bqhc,bkhc->bhqk", queries, key_rows, preferred_element_type=jnp.float32
    ) / math.sqrt(HEAD_IMG)
    probabilities = softmax_rows(scores)
    attended = jnp.einsum(
        "bhqk,bkhc->bqhc", probabilities, value_rows, preferred_element_type=jnp.float32
    ).astype(jnp.bfloat16)
    attended = attended.reshape(item_count, patch_count, half_width)
    projected = jnp.einsum("bpc,cd->bpd", attended, w_out, preferred_element_type=jnp.float32)
    return jnp.mean(projected, axis=1)


def text_attention(texts, flat_slot):
    item_count, token_count, model_width = texts.shape
    half_width = model_width // 2
    head_count = half_width // HEAD_TXT
    inner_width = half_width + 2 * HEAD_TXT
    qkv_size = model_width * inner_width
    w_qkv = flat_slot[:qkv_size].reshape(model_width, inner_width)
    w_out = flat_slot[qkv_size : qkv_size + half_width * model_width].reshape(
        half_width, model_width
    )
    float_tokens = texts.astype(jnp.float32)
    normed = (
        float_tokens
        * lax.rsqrt(jnp.mean(float_tokens * float_tokens, axis=-1, keepdims=True) + norm_eps)
    ).astype(jnp.bfloat16)
    projections = jnp.einsum("btd,de->bte", normed, w_qkv, preferred_element_type=jnp.float32)
    positions = jnp.arange(token_count).astype(jnp.float32)
    queries = rotate_pairs(
        projections[..., :half_width].reshape(item_count, token_count, head_count, HEAD_TXT),
        positions,
    ).astype(jnp.bfloat16)
    key_rows = rotate_pairs(
        projections[..., half_width : half_width + HEAD_TXT].reshape(
            item_count, token_count, 1, HEAD_TXT
        ),
        positions,
    )[:, :, 0, :].astype(jnp.bfloat16)
    value_rows = projections[..., half_width + HEAD_TXT :].astype(jnp.bfloat16)
    scores = jnp.einsum(
        "bqhc,bkc->bhqk", queries, key_rows, preferred_element_type=jnp.float32
    ) / math.sqrt(HEAD_TXT)
    causal = jnp.arange(token_count)[:, None] >= jnp.arange(token_count)[None, :]
    scores = jnp.where(causal, scores, -1e30)
    probabilities = softmax_rows(scores)
    attended = jnp.einsum(
        "bhqk,bkc->bqhc", probabilities, value_rows, preferred_element_type=jnp.float32
    ).astype(jnp.bfloat16)
    attended = attended.reshape(item_count, token_count, half_width)
    projected = jnp.einsum("btc,cd->btd", attended, w_out, preferred_element_type=jnp.float32)
    return jnp.mean(projected, axis=1)


def merge_forward(embedded, stacked):
    first_rows = embedded.shape[1]
    float_embed = embedded.astype(jnp.float32)
    normed = (
        float_embed
        * lax.rsqrt(jnp.mean(float_embed * float_embed, axis=1, keepdims=True) + norm_eps)
    ).astype(jnp.bfloat16)
    hidden = jnp.dot(normed, stacked[:first_rows], preferred_element_type=jnp.float32)
    activated = gelu_value(hidden).astype(jnp.bfloat16)
    merged = jnp.dot(activated, stacked[first_rows:], preferred_element_type=jnp.float32).astype(
        jnp.bfloat16
    )
    return (normed, hidden, activated, merged)


def merge_backward(hidden, stacked, out_grad, first_rows):
    w_second = stacked[first_rows:]
    act_grad = lax.dot_general(
        out_grad, w_second, (((1,), (1,)), ((), ())), preferred_element_type=jnp.float32
    )
    return (act_grad * gelu_slope(hidden)).astype(jnp.bfloat16)


def item_loss(merged_row, book_rows, negatives):
    emb_width = merged_row.shape[0]
    quant_tau = math.sqrt(emb_width) / 2.0
    residual = merged_row * lax.rsqrt(jnp.mean(merged_row * merged_row) + norm_eps)
    quantized = jnp.zeros_like(merged_row)
    for level_index in range(book_rows.shape[0]):
        code_rows = book_rows[level_index]
        cross_terms = jnp.dot(code_rows, residual, precision=highest)
        logits = (2.0 * cross_terms - jnp.sum(code_rows * code_rows, axis=1)) / quant_tau
        logits = logits - lax.stop_gradient(jnp.max(logits))
        exp_logits = jnp.exp(logits)
        chosen = jnp.dot(exp_logits / jnp.sum(exp_logits), code_rows, precision=highest)
        residual = residual - chosen
        quantized = quantized + chosen
    recon_error = jnp.mean(residual * residual)
    anchor = quantized * lax.rsqrt(jnp.mean(quantized * quantized) + norm_eps)
    candidates = jnp.concatenate([merged_row[None, :], negatives.astype(jnp.float32)], axis=0)
    cand_unit = candidates * lax.rsqrt(
        jnp.mean(candidates * candidates, axis=1, keepdims=True) + norm_eps
    )
    similarity = jnp.dot(cand_unit, anchor, precision=highest) / (emb_width * contrast_temp)
    top_score = lax.stop_gradient(jnp.max(similarity))
    contrast = top_score + jnp.log(jnp.sum(jnp.exp(similarity - top_score))) - similarity[0]
    return contrast + beta_weight * recon_error


def stacked_term(columns, first_grad, second_grad, in_first):
    contract = (((0,), (0,)), ((), ()))
    first_term = lax.dot_general(columns, first_grad, contract, preferred_element_type=jnp.float32)
    second_term = lax.dot_general(
        columns, second_grad, contract, preferred_element_type=jnp.float32
    )
    return jnp.where(in_first[:, None], first_term, second_term)


def per_device(
    images,
    texts,
    section_weights,
    uniting_weights,
    codebooks,
    neg_bank,
    item_cats,
    cat_slot,
    neg_index,
):
    segment_index = lax.axis_index("segment")
    segment_count = lax.axis_size("segment")
    dp_index = lax.axis_index("dp")
    dp_count = lax.axis_size("dp")
    group_index = segment_index % 2
    item_count = images.shape[0]
    flat_slot = section_weights.reshape(-1)
    residual_flag = jnp.where(group_index == 0, 1.0, 0.0).astype(jnp.float32)

    def image_branch(operands):
        image_rows, text_rows, slot_rows = operands
        pooled = image_attention(image_rows, slot_rows) + residual_flag * jnp.mean(
            image_rows.astype(jnp.float32), axis=1
        )
        return jnp.concatenate(
            [pooled, jnp.zeros((item_count, text_rows.shape[2]), jnp.float32)], axis=1
        )

    def text_branch(operands):
        image_rows, text_rows, slot_rows = operands
        pooled = text_attention(text_rows, slot_rows) + residual_flag * jnp.mean(
            text_rows.astype(jnp.float32), axis=1
        )
        return jnp.concatenate(
            [jnp.zeros((item_count, image_rows.shape[2]), jnp.float32), pooled], axis=1
        )

    packed = lax.cond(segment_index < 2, image_branch, text_branch, (images, texts, flat_slot))
    embedded = lax.psum_scatter(packed, "segment", scatter_dimension=0, tiled=True).astype(
        jnp.bfloat16
    )
    stacked = lax.all_gather(uniting_weights, "dp", axis=0, tiled=True)
    first_rows = embedded.shape[1]
    cat_per_dev = codebooks.shape[0]
    slot_count = cat_per_dev * CAP
    row_total = item_cats.shape[1]
    cats_all = item_cats.reshape(-1)
    entry_count = cats_all.shape[0]
    entry_ids = jnp.arange(entry_count)
    category_match = cats_all[:, None] == jnp.arange(cat_slot.shape[0])[None, :]
    entry_slots = jnp.sum(jnp.where(category_match, cat_slot[None, :], 0), axis=1)
    entry_owner = entry_slots // cat_per_dev
    entry_local = entry_slots % cat_per_dev
    entry_row = entry_ids // row_total
    earlier = entry_ids[None, :] < entry_ids[:, None]
    same_cat = (cats_all[:, None] == cats_all[None, :]) & (entry_row[:, None] == entry_row[None, :])
    entry_rank = jnp.sum(jnp.where(earlier & same_cat, 1, 0), axis=1)
    entry_place = entry_local * CAP + entry_rank
    entry_position = entry_row * slot_count + entry_place
    owned = entry_owner == dp_index
    all_slots = segment_count * slot_count
    slot_match_all = owned[None, :] & (entry_position[None, :] == jnp.arange(all_slots)[:, None])
    view_match = lax.dynamic_slice(
        slot_match_all,
        (segment_index * slot_count, segment_index * row_total),
        (slot_count, row_total),
    )
    view_base = segment_index * row_total
    view_slots = view_match.shape[0]
    selection = view_match.astype(jnp.bfloat16)
    valid = jnp.sum(view_match.astype(jnp.float32), axis=1)
    slot_item = jnp.sum(
        jnp.where(view_match, jnp.arange(view_match.shape[1])[None, :] + view_base, 0), axis=1
    )
    slot_negs = jnp.take(neg_index.reshape(entry_count, -1), slot_item, axis=0)
    slot_local = jnp.arange(view_slots) % slot_count // CAP
    bank_rows = neg_bank.reshape(-1, neg_bank.shape[2])
    negatives = jnp.take(bank_rows, slot_local[:, None] * neg_bank.shape[1] + slot_negs, axis=0)
    loss_scale = 1.0 / math.sqrt(dp_count * item_count)

    def owner_objective(merged_float, books):
        per_row = jax.vmap(item_loss)(merged_float, books[slot_local], negatives)
        return jnp.sum(per_row * valid) * loss_scale

    gathered = jnp.dot(
        selection,
        lax.all_gather(embedded, "dp", axis=0, tiled=True),
        preferred_element_type=jnp.float32,
    )
    gathered = gathered.astype(jnp.bfloat16)
    normed_all, hidden_all, activated_all, merged_all = merge_forward(gathered, stacked)
    loss_local, pullback = jax.vjp(owner_objective, merged_all.astype(jnp.float32), codebooks)
    grad_all, book_grad = pullback(jnp.ones((), jnp.float32))
    out_grad = grad_all.astype(jnp.bfloat16)
    hidden_grad = merge_backward(hidden_all, stacked, out_grad, first_rows)
    joined = jnp.concatenate([normed_all, activated_all], axis=1)
    book_total, loss_owner = lax.psum((book_grad, loss_local), "segment")
    shard_rows = uniting_weights.shape[0]
    shard_start = dp_index * shard_rows
    shard_first = shard_start + jnp.arange(shard_rows) < first_rows
    joined_piece = lax.all_gather(joined, "dp", axis=0, tiled=True)
    first_piece = lax.all_gather(hidden_grad, "dp", axis=0, tiled=True)
    second_piece = lax.all_gather(out_grad, "dp", axis=0, tiled=True)
    columns = lax.dynamic_slice_in_dim(joined_piece, shard_start, shard_rows, 1)
    segment_grad = stacked_term(columns, first_piece, second_piece, shard_first)
    uniting_grad = lax.psum(segment_grad, "segment")
    return (uniting_grad, book_total, loss_owner.reshape(1))


def solution(mesh):
    placed = (
        P("dp", None, None),
        P("dp", None, None),
        P("segment", None, None),
        P("dp", None),
        P("dp", None, None, None),
        P("dp", None, None),
        P(),
        P(),
        P(),
    )
    return jax.shard_map(
        per_device,
        mesh=mesh,
        in_specs=placed,
        out_specs=(P("dp", None), P("dp", None, None, None), P("dp")),
        check_vma=False,
    )
```

profile of v0, /device:TPU:1, one launch (start us, length us, event | category | flops | bytes accessed | tf_op | source)
XLA Modules:
  0.0 945.5 jit_solution(2078119373908854478)
XLA Ops:
  9.9 64.5 %conditional.1 = (f32[8,2560]{1,0:T(8,128)S(1)}) conditional(s32[]{:T(128)} %convert_element_type.98, (bf16[8,64,1536]{2,1,0:T(8,128)(2,1)}, bf16[2752512]{0:T(1024)(128)(2,1)}, f32[]{:T(128)}) %tuple.55, (bf16[8,256,1024]{2,1,0:T(8,128)(2,1)}, bf16[2752512]{0:T(1024)(128)(2,1)}, f32[]{:T(128)}) %tuple.56), branch_computations={%region_2.8_spmd, %region_8.15_spmd} | conditional | flops 9714018304 | bytes 131555384 | solution.py:217
  10.4 3.0 convert_reduce_fusion.2
  13.4 3.5 fusion.43
  18.7 6.8 reshape.489
  25.5 9.9 %convolution_convert_fusion.1 = bf16[8,256,1536]{2,1,0:T(8,128)(2,1)S(1)} fusion(bf16[1024,1536,1]{1,0,2:T(8,128)(2,1)} %reshape.489, bf16[8,256,1024]{2,1,0:T(8,128)(2,1)} %get-tuple-element.27, f32[8,256]{1,0:T(8,128)S(1)} %add_rsqrt_fusion.1, f32[8,256]{1,0:T(8,128)S(1)} %broadcast_multiply_fusion), kind=kOutput, calls=%fused_computation.65 | convolution fusion | flops 6453985280 | bytes 13647872 | tf_op jit(solution)/shard_map/cond/branch_1_fun/bpd,de->bpe/dot_general | solution.py:57
  35.4 2.8 fusion.168
  38.2 4.0 copy.70
  42.2 3.9 copy.71
  46.1 10.6 %fusion.169 = (f32[8,8,256]{2,1,0:T(8,128)S(1)}, f32[8,8,256,256]{2,3,1,0:T(8,128)}) fusion(bf16[8,256,8,64]{1,3,2,0:T(8,128)(2,1)} %bitcast.232, bf16[8,256,8,64]{1,3,2,0:T(8,128)(2,1)} %bitcast.233), kind=kOutput, calls=%fused_computation.284 | convolution fusion | flops 549454080 | bytes 21037056 | tf_op jit(solution)/shard_map/cond/branch_1_fun/sub | solution.py:39
  56.7 2.4 copy.69
  59.1 9.4 fusion.52
  70.2 4.0 convolution_reduce_fusion.1
  74.5 13.8 %all-reduce.5 = bf16[8,2560]{1,0:T(8,128)(2,1)S(1)} all-reduce(f32[8,2560]{1,0:T(8,128)S(1)} %get-tuple-element.92), channel_id=2, replica_groups=mesh['segment'=4,'dp'=64] {'segment'}, use_global_device_ids=true, to_apply=%region_15.16.clone | all-reduce | flops 20480 | bytes 122880
  88.3 160.0 %all-gather = bf16[64,2,2560]{2,1,0:T(2,128)(2,1)S(1)} all-gather(bf16[1,2,2560]{2,1,0:T(2,128)(2,1)S(1)} %fusion.106), channel_id=1, replica_groups=mesh['segment'=4,'dp'=64] {'dp'}, dimensions={0}, use_global_device_ids=true | all-gather | bytes 665600 | tf_op jit(solution)/shard_map/all_gather | solution.py:266
  256.9 3.3 multiply_convert_fusion.1
  293.3 2.2 fusion.77
  295.5 148.0 %all-gather.2 = bf16[64,2,1024]{2,1,0:T(2,128)(2,1)S(1)} all-gather(bf16[1,2,1024]{2,1,0:T(2,128)(2,1)S(1)} %fusion.77), channel_id=1, replica_groups=mesh['segment'=4,'dp'=64] {'dp'}, dimensions={0}, use_global_device_ids=true | all-gather | bytes 266240 | tf_op jit(solution)/shard_map/all_gather | solution.py:281
  444.4 155.0 %all-gather.1 = bf16[64,2,3584]{2,1,0:T(2,128)(2,1)S(1)} all-gather(bf16[1,2,3584]{2,1,0:T(2,128)(2,1)} %maximum_bitcast_fusion), channel_id=1, replica_groups=mesh['segment'=4,'dp'=64] {'dp'}, dimensions={0}, use_global_device_ids=true | all-gather | bytes 931840 | tf_op jit(solution)/shard_map/all_gather | solution.py:280
  600.7 148.5 %all-gather.3 = bf16[64,2,1024]{2,1,0:T(2,128)(2,1)S(1)} all-gather(bf16[1,2,1024]{2,1,0:T(2,128)(2,1)} %bitcast.244), channel_id=1, replica_groups=mesh['segment'=4,'dp'=64] {'dp'}, dimensions={0}, use_global_device_ids=true | all-gather | bytes 266240 | tf_op jit(solution)/shard_map/all_gather | solution.py:282
  751.2 2.2 pad_add_fusion
  754.0 4.5 scatter_fusion
  763.6 116.9 %psum.23 = f32[1]{0:T(128)} all-reduce(f32[1]{0:T(128)} %bitcast.57), channel_id=1, replica_groups=mesh['segment'=4,'dp'=64] {'segment'}, use_global_device_ids=true, to_apply=%region_40.41 | all-reduce | flops 1 | bytes 8 | tf_op jit(solution)/shard_map/psum | solution.py:276
  880.5 53.2 %all-reduce.9.cloned.1.call-done = (f32[56,1024]{1,0:T(8,128)}, f32[1,2,256,1024]{3,2,1,0:T(8,128)}) async-done(((f32[56,1024]{1,0:T(8,128)}, f32[1,2,256,1024]{3,2,1,0:T(8,128)}), (f32[56,1024]{1,0:T(8,128)}, f32[1,2,256,1024]{3,2,1,0:T(8,128)})) %all-reduce.9.cloned.1.call-update) | async-done | bytes 2326544 | tf_op jit(solution)/shard_map/psum | solution.py:285
  935.3 3.2 copy.190
  (175 shorter events, 57.6 us)
Async XLA Ops:
  7.2 244.2 %copy-start = (bf16[1,256,1024]{2,1,0:T(8,128)(2,1)S(1)}, bf16[1,256,1024]{2,1,0:T(8,128)(2,1)}, u32[]{:S(2)}) copy-start(bf16[1,256,1024]{2,1,0:T(8,128)(2,1)} %param.16) | copy-start | bytes 1572868
  7.2 249.7 %all-gather.6.cloned.1.call-start = ((), (), s32[]{:S(2)}) async-start(), calls=%async_computation | async-start | bytes 7454720 | tf_op jit(solution)/shard_map/all_gather | solution.py:221
  7.9 925.8 %all-reduce.9.cloned.1.call-start = ((), (), s32[]{:S(2)}) async-start(), calls=%async_computation.1 | async-start | bytes 4653056 | tf_op jit(solution)/shard_map/psum | solution.py:285
  10.4 6.5 copy-start.4
  74.4 174.1 %copy-start.15 = (s32[4,128,1]{1,2,0:T(1,128)S(1)}, s32[4,128,1]{1,2,0:T(1,128)}, u32[]{:S(2)}) copy-start(s32[4,128,1]{1,2,0:T(1,128)} %param.17) | copy-start | bytes 6148
  74.5 174.1 %copy-start.28 = (s32[64]{0:T(128)S(1)}, s32[64]{0:T(128)}, u32[]{:S(2)}) copy-start(s32[64]{0:T(128)} %param.18) | copy-start | bytes 772
  249.4 27.3 %copy-start.24 = (f32[2]{0:T(128)}, f32[2]{0:T(128)S(1)}, u32[]{:S(2)}) copy-start(f32[2]{0:T(128)S(1)} %get-tuple-element.44) | copy-start | bytes 28
  262.3 8.6 copy-start.2
  271.8 8.5 copy-start.11
  276.6 10.7 %copy-start.17 = (f32[2]{0:T(128)}, f32[2]{0:T(128)S(1)}, u32[]{:S(2)}) copy-start(f32[2]{0:T(128)S(1)} %get-tuple-element.72) | copy-start | bytes 28
  278.0 10.7 %copy-start.3 = (f32[2,128,1024]{2,0,1:T(2,128)S(1)}, f32[2,128,1024]{2,0,1:T(2,128)}, u32[]{:S(2)}) copy-start(f32[2,128,1024]{2,0,1:T(2,128)} %fusion.101) | copy-start | bytes 3145732
  285.6 6.2 copy-start.12
  285.6 6.3 slice-start
  600.7 149.9 %copy-start.13 = (f32[2,1024]{1,0:T(2,128)S(1)}, f32[2,1024]{1,0:T(2,128)}, u32[]{:S(2)}) copy-start(f32[2,1024]{1,0:T(2,128)} %copy-done.12) | copy-start | bytes 24580
  600.7 149.9 %copy-start.14 = (f32[2,1024]{1,0:T(2,128)S(1)}, f32[2,1024]{1,0:T(2,128)}, u32[]{:S(2)}) copy-start(f32[2,1024]{1,0:T(2,128)} %broadcast_multiply_fusion.4) | copy-start | bytes 24580
  600.7 149.9 %copy-start.19 = (f32[2,256]{1,0:T(2,128)S(1)}, f32[2,256]{1,0:T(2,128)}, u32[]{:S(2)}) copy-start(f32[2,256]{1,0:T(2,128)} %get-tuple-element.76) | copy-start | bytes 6148
  600.7 149.9 %copy-start.20 = (f32[2,256]{1,0:T(2,128)S(1)}, f32[2,256]{1,0:T(2,128)}, u32[]{:S(2)}) copy-start(f32[2,256]{1,0:T(2,128)} %broadcast_divide_fusion.1) | copy-start | bytes 6148
  600.7 149.9 %copy-start.21 = (f32[2,256]{1,0:T(2,128)S(1)}, f32[2,256]{1,0:T(2,128)}, u32[]{:S(2)}) copy-start(f32[2,256]{1,0:T(2,128)} %get-tuple-element.38) | copy-start | bytes 6148
  754.0 4.5 copy-start.10
  754.0 5.8 copy-start.29
  758.5 3.2 copy-start.18
  758.5 3.2 copy-start.23
  758.5 3.2 copy-start.25
  758.5 3.2 copy-start.26
  (8 other events, 12.8 us)
Sparse Core Ops, SparseCore 0:
  11.5 144.8 all-gather.5
  761.8 171.8 all-reduce.8
where the time goes:
time: 953 us; the launch traced here: 946 us
  blocking collectives  742 us (78%)
  matrix products  59.7 us (6%)
  waiting for transfers between devices  53.9 us (6%)
  local copies, waits for them, and re-layouts  39.2 us (4%)
  other arithmetic  33.6 us (4%)
  between operations  16.1 us (2%)
    all_gather x1, blocking collectives, per_device(): lax.all_gather(embedded, 'dp', axis=0, tiled=True)  160 us
    all_gather x1, blocking collectives, per_device(): joined_piece = lax.all_gather(joined, 'dp', axis=0, tiled=True)  155 us
    all_gather x1, blocking collectives, per_device(): second_piece = lax.all_gather(out_grad, 'dp', axis=0, tiled=True)  149 us
    all_gather x1, blocking collectives, per_device(): first_piece = lax.all_gather(hidden_grad, 'dp', axis=0, tiled=True)  148 us
    psum x1, blocking collectives, per_device(): book_total, loss_owner = lax.psum((book_grad, loss_local), 'segment')  117 us
    psum x1, waiting for transfers between devices, per_device(): uniting_grad = lax.psum(segment_grad, 'segment')  53.2 us
  transfers between devices with their start and end apart: 2, of which 1 were waited for; matrix products, arithmetic and copies ran while one was open for 8% of the time, Pallas kernels for 0%

commit v1 on v0

--- a/solution.py
+++ b/solution.py
@@ -282,7 +282,7 @@
     second_piece = lax.all_gather(out_grad, "dp", axis=0, tiled=True)
     columns = lax.dynamic_slice_in_dim(joined_piece, shard_start, shard_rows, 1)
     segment_grad = stacked_term(columns, first_piece, second_piece, shard_first)
-    uniting_grad = lax.psum(segment_grad, "segment")
+    uniting_grad = jax.lax.all_gather(segment_grad, "segment").sum(axis=0)
     return (uniting_grad, book_total, loss_owner.reshape(1))
 
 

time: 953 us -> 900 us (0.944)
  waiting for transfers between devices: 53.9 us -> 0.72 us
    all_gather x0 -> x1, blocking collectives: none -> 91.8 us  [per_device(): uniting_grad = jax.lax.all_gather(segment_grad, 'segment').sum(axis=0)]
    psum x1, blocking collectives: 117 us -> 34.7 us  [per_device(): book_total, loss_owner = lax.psum((book_grad, loss_local), 'segment')]
    psum x1, waiting for transfers between devices: 53.2 us -> 0.01 us  [per_device(): book_total, loss_owner = lax.psum((book_grad, loss_local), 'segment')]
  transfers between devices with their start and end apart: 2 -> 2, of which waited for: 1 -> 0; matrix products, arithmetic and copies ran while one was open for 8% -> 9% of each run, Pallas kernels for 0% -> 0%
where the time goes in v1:
time: 900 us; the launch traced here: 893 us
  blocking collectives  751 us (83%)
  matrix products  57.1 us (6%)
  local copies, waits for them, and re-layouts  37.4 us (4%)
  other arithmetic  29.7 us (3%)
  between operations  16 us (2%)
    all_gather x1, blocking collectives, per_device(): lax.all_gather(embedded, 'dp', axis=0, tiled=True)  160 us
    all_gather x1, blocking collectives, per_device(): joined_piece = lax.all_gather(joined, 'dp', axis=0, tiled=True)  155 us
    all_gather x1, blocking collectives, per_device(): first_piece = lax.all_gather(hidden_grad, 'dp', axis=0, tiled=True)  148 us
    all_gather x1, blocking collectives, per_device(): second_piece = lax.all_gather(out_grad, 'dp', axis=0, tiled=True)  148 us
    all_gather x1, blocking collectives, per_device(): uniting_grad = jax.lax.all_gather(segment_grad, 'segment').sum(axis=0)  91.8 us
    psum x1, blocking collectives, per_device(): book_total, loss_owner = lax.psum((book_grad, loss_local), 'segment')  34.7 us
  transfers between devices with their start and end apart: 2, of which 0 were waited for; matrix products, arithmetic and copies ran while one was open for 9% of the time, Pallas kernels for 0%

profile of v1, /device:TPU:1, one launch (start us, length us, event | category | flops | bytes accessed | tf_op | source)
XLA Modules:
  0.0 893.1 jit_solution(15912746876364897428)
XLA Ops:
  9.9 64.5 %conditional.1 = (f32[8,2560]{1,0:T(8,128)S(1)}) conditional(s32[]{:T(128)} %convert_element_type.98, (bf16[8,64,1536]{2,1,0:T(8,128)(2,1)}, bf16[2752512]{0:T(1024)(128)(2,1)}, f32[]{:T(128)}) %tuple.54, (bf16[8,256,1024]{2,1,0:T(8,128)(2,1)}, bf16[2752512]{0:T(1024)(128)(2,1)}, f32[]{:T(128)}) %tuple.55), branch_computations={%region_2.8_spmd, %region_8.15_spmd} | conditional | flops 9714018304 | bytes 131555384 | solution.py:217
  10.4 3.0 convert_reduce_fusion.2
  13.4 3.5 fusion.43
  18.7 6.8 reshape.490
  25.5 9.9 %convolution_convert_fusion.1 = bf16[8,256,1536]{2,1,0:T(8,128)(2,1)S(1)} fusion(bf16[1024,1536,1]{1,0,2:T(8,128)(2,1)} %reshape.490, bf16[8,256,1024]{2,1,0:T(8,128)(2,1)} %get-tuple-element.27, f32[8,256]{1,0:T(8,128)S(1)} %add_rsqrt_fusion.1, f32[8,256]{1,0:T(8,128)S(1)} %broadcast_multiply_fusion), kind=kOutput, calls=%fused_computation.65 | convolution fusion | flops 6453985280 | bytes 13647872 | tf_op jit(solution)/shard_map/cond/branch_1_fun/bpd,de->bpe/dot_general | solution.py:57
  35.4 2.8 fusion.168
  38.2 4.0 copy.70
  42.2 3.9 copy.71
  46.1 10.6 %fusion.169 = (f32[8,8,256]{2,1,0:T(8,128)S(1)}, f32[8,8,256,256]{2,3,1,0:T(8,128)}) fusion(bf16[8,256,8,64]{1,3,2,0:T(8,128)(2,1)} %bitcast.234, bf16[8,256,8,64]{1,3,2,0:T(8,128)(2,1)} %bitcast.235), kind=kOutput, calls=%fused_computation.284 | convolution fusion | flops 549454080 | bytes 21037056 | tf_op jit(solution)/shard_map/cond/branch_1_fun/sub | solution.py:39
  56.7 2.4 copy.69
  59.0 9.4 %fusion.52 = bf16[8,8,64,256]{3,2,1,0:T(8,128)(2,1)} fusion(bf16[8,256,8,64]{1,3,2,0:T(8,128)(2,1)} %bitcast.236, f32[8,8,256,256]{2,3,1,0:T(8,128)} %get-tuple-element.64, f32[8,8,256]{2,1,0:T(8,128)S(1)} %get-tuple-element.63), kind=kOutput, calls=%fused_computation.70 | convolution fusion | flops 546308096 | bytes 21037056 | tf_op jit(solution)/shard_map/cond/branch_1_fun/bhqk,bkhc->bqhc/dot_general | solution.py:71
  70.2 4.0 convolution_reduce_fusion.1
  74.4 13.8 %all-reduce.5 = bf16[8,2560]{1,0:T(8,128)(2,1)S(1)} all-reduce(f32[8,2560]{1,0:T(8,128)S(1)} %get-tuple-element.88), channel_id=3, replica_groups=mesh['segment'=4,'dp'=64] {'segment'}, use_global_device_ids=true, to_apply=%region_15.16.clone | all-reduce | flops 20480 | bytes 122880
  88.3 160.0 %all-gather.1 = bf16[64,2,2560]{2,1,0:T(2,128)(2,1)S(1)} all-gather(bf16[1,2,2560]{2,1,0:T(2,128)(2,1)S(1)} %fusion.106), channel_id=1, replica_groups=mesh['segment'=4,'dp'=64] {'dp'}, dimensions={0}, use_global_device_ids=true | all-gather | bytes 665600 | tf_op jit(solution)/shard_map/all_gather | solution.py:266
  256.3 3.3 multiply_convert_fusion.1
  281.0 34.7 %psum.15 = f32[1]{0:T(128)} all-reduce(f32[1]{0:T(128)} %bitcast.58), channel_id=1, replica_groups=mesh['segment'=4,'dp'=64] {'segment'}, use_global_device_ids=true, to_apply=%region_40.41 | all-reduce | flops 1 | bytes 8 | tf_op jit(solution)/shard_map/psum | solution.py:276
  318.8 2.2 pad_add_fusion
  322.6 8.0 scatter_fusion
  335.9 2.2 fusion.77
  338.1 148.5 %all-gather.3 = bf16[64,2,1024]{2,1,0:T(2,128)(2,1)S(1)} all-gather(bf16[1,2,1024]{2,1,0:T(2,128)(2,1)S(1)} %fusion.77), channel_id=1, replica_groups=mesh['segment'=4,'dp'=64] {'dp'}, dimensions={0}, use_global_device_ids=true | all-gather | bytes 266240 | tf_op jit(solution)/shard_map/all_gather | solution.py:281
  486.7 154.5 %all-gather.2 = bf16[64,2,3584]{2,1,0:T(2,128)(2,1)S(1)} all-gather(bf16[1,2,3584]{2,1,0:T(2,128)(2,1)S(1)} %maximum_bitcast_fusion), channel_id=1, replica_groups=mesh['segment'=4,'dp'=64] {'dp'}, dimensions={0}, use_global_device_ids=true | all-gather | bytes 931840 | tf_op jit(solution)/shard_map/all_gather | solution.py:280
  641.6 148.0 %all-gather.4 = bf16[64,2,1024]{2,1,0:T(2,128)(2,1)S(1)} all-gather(bf16[1,2,1024]{2,1,0:T(2,128)(2,1)S(1)} %bitcast.246), channel_id=1, replica_groups=mesh['segment'=4,'dp'=64] {'dp'}, dimensions={0}, use_global_device_ids=true | all-gather | bytes 266240 | tf_op jit(solution)/shard_map/all_gather | solution.py:282
  790.3 91.8 %all-gather = f32[224,1024]{1,0:T(8,128)S(1)} all-gather(f32[56,1024]{1,0:T(8,128)S(1)} %convolution_select_fusion), channel_id=2, replica_groups=mesh['segment'=4,'dp'=64] {'segment'}, dimensions={0}, use_global_device_ids=true | all-gather | bytes 1146880 | tf_op jit(solution)/shard_map/all_gather | solution.py:285
  882.8 3.2 copy.188
  (140 shorter events, 45.8 us)
Async XLA Ops:
  7.2 244.2 %copy-start = (bf16[1,256,1024]{2,1,0:T(8,128)(2,1)S(1)}, bf16[1,256,1024]{2,1,0:T(8,128)(2,1)}, u32[]{:S(2)}) copy-start(bf16[1,256,1024]{2,1,0:T(8,128)(2,1)} %param.16) | copy-start | bytes 1572868
  7.2 249.1 %all-gather.7.cloned.1.call-start = ((), (), s32[]{:S(2)}) async-start(), calls=%async_computation | async-start | bytes 7454720 | tf_op jit(solution)/shard_map/all_gather | solution.py:221
  7.9 874.9 %all-reduce.8.cloned.1.call-start = ((), (), s32[]{:S(2)}) async-start(), calls=%async_computation.1 | async-start | bytes 4194304 | tf_op jit(solution)/shard_map/psum | solution.py:276
  10.4 6.5 copy-start.3
  74.4 174.2 %copy-start.11 = (s32[4,128,1]{1,2,0:T(1,128)S(1)}, s32[4,128,1]{1,2,0:T(1,128)}, u32[]{:S(2)}) copy-start(s32[4,128,1]{1,2,0:T(1,128)} %param.17) | copy-start | bytes 6148
  74.4 174.2 %copy-start.12 = (s32[64]{0:T(128)S(1)}, s32[64]{0:T(128)}, u32[]{:S(2)}) copy-start(s32[64]{0:T(128)} %param.18) | copy-start | bytes 772
  251.3 2.0 copy-start.5
  253.3 1.0 copy-start.7
  253.4 2.6 copy-start.6
  261.8 6.8 copy-start.1
  269.5 6.6 copy-start.10
  271.3 1.0 copy-start.4
  330.7 1.2 copy-start.2
  331.9 3.2 slice-start
Sparse Core Ops, SparseCore 0:
  11.5 144.8 all-gather.6
  330.8 57.1 all-reduce.7
